TPU v7x, 32 devices: a whole 2x2x4 slice. The times are simulated.
32 devices in a mesh: tp: 8 (over z, y), dp: 4 (over x, core).
Axes of the slice: x: 2, y: 2, z: 4, core: 2. Of those that a mesh axis runs over, the one named last changes fastest.
Arguments:
- tokens: bfloat16 [4, 16, 4096], P('dp', 'tp'), may hold values from -6 to 6
- gate_weight: bfloat16 [4096, 16384], P('dp', 'tp'), may hold values from -0.09375 to 0.09375
- up_weight: bfloat16 [4096, 16384], P('dp', 'tp'), may hold values from -0.09375 to 0.09375
- cotangent: bfloat16 [4, 16, 16384], P('dp', None, 'tp'), may hold values from -6 to 6
Outputs:
- hidden: bfloat16 [4, 16, 16384], P('dp', None, 'tp')
- grad_tokens: bfloat16 [4, 16, 4096], P('dp', 'tp')
- grad_gate: bfloat16 [4096, 16384], P(None, 'tp')
- grad_up: bfloat16 [4096, 16384], P(None, 'tp')
All inputs are finite; a program needn't handle non-finite values.
Results may differ from a plain program's by a relative error of at most 0.009.
Values may be sent and summed in bfloat16 or wider, within the bound.
No kernel may reach another device: no remote copies, remote signals or barrier semaphores. Data moves between devices by JAX's collectives and lax.ppermute only.
A program may use at most 320 MiB of HBM per device.

v0:
```python
import jax
import jax.numpy as jnp
from jax import lax
from jax.sharding import PartitionSpec as P


def swish_parts(gate_pre):
    sigmoid_val = jax.nn.sigmoid(gate_pre)
    return (gate_pre * sigmoid_val, sigmoid_val * (1.0 + gate_pre * (1.0 - sigmoid_val)))


def shards(tokens, gate_weight, up_weight, cotangent):
    gate_full, up_full = (
        lax.all_gather(gate_weight, "dp", axis=0, tiled=True),
        lax.all_gather(up_weight, "dp", axis=0, tiled=True),
    )
    gathered = lax.all_gather(tokens, "tp", axis=1, tiled=True)
    flat_rows = gathered[0]
    gate_pre = jnp.dot(flat_rows, gate_full, preferred_element_type=jnp.float32)
    up_pre = jnp.dot(flat_rows, up_full, preferred_element_type=jnp.float32)
    swish_act, swish_slope = swish_parts(gate_pre)
    hidden = (swish_act * up_pre).astype(jnp.bfloat16)
    back_float = cotangent[0].astype(jnp.float32)
    d_gate = (back_float * up_pre * swish_slope).astype(jnp.bfloat16)
    d_up = (back_float * swish_act).astype(jnp.bfloat16)
    across = (((1,), (1,)), ((), ()))
    down_rows = (((0,), (0,)), ((), ()))
    result = lax.dot_general(d_gate, gate_full, across, preferred_element_type=jnp.float32)
    grad_rows = lax.psum_scatter(
        result + lax.dot_general(d_up, up_full, across, preferred_element_type=jnp.float32),
        "tp",
        scatter_dimension=0,
        tiled=True,
    )
    grad_tokens = grad_rows.astype(jnp.bfloat16)[None]
    inverse_dp = 1.0 / lax.axis_size("dp")
    rows_p = lax.all_gather(gathered, "dp", axis=0, tiled=True)
    gate_p = lax.all_gather(d_gate[None], "dp", axis=0, tiled=True)
    up_p = lax.all_gather(d_up[None], "dp", axis=0, tiled=True)
    acc_gate = jnp.zeros(gate_full.shape, jnp.float32)
    acc_up = jnp.zeros(up_full.shape, jnp.float32)
    for replica in range(rows_p.shape[0]):
        term_gate = lax.dot_general(
            rows_p[replica], gate_p[replica], down_rows, preferred_element_type=jnp.float32
        )
        term_up = lax.dot_general(
            rows_p[replica], up_p[replica], down_rows, preferred_element_type=jnp.float32
        )
        acc_gate = acc_gate + lax.optimization_barrier(term_gate.astype(jnp.bfloat16)).astype(
            jnp.float32
        )
        acc_up = acc_up + lax.optimization_barrier(term_up.astype(jnp.bfloat16)).astype(jnp.float32)
    grad_gate = (acc_gate * inverse_dp).astype(jnp.bfloat16)
    grad_up = (acc_up * inverse_dp).astype(jnp.bfloat16)
    return (hidden[None], grad_tokens, grad_gate, grad_up)


def solution(mesh):
    in_specs = (P("dp", "tp", None), P("dp", "tp"), P("dp", "tp"), P("dp", None, "tp"))
    out_specs = (P("dp", None, "tp"), P("dp", "tp", None), P(None, "tp"), P(None, "tp"))
    return jax.shard_map(shards, mesh=mesh, in_specs=in_specs, out_specs=out_specs, check_vma=False)
```

profile of v0, /device:TPU:0, one launch (start us, length us, event | category | flops | bytes accessed | tf_op | source)
XLA Modules:
  0.0 485.2 jit_solution(3672661935274794439)
XLA Ops:
  7.2 0.0 copy-start
  7.2 0.0 all-gather.7.cloned.1.call-start
  7.2 0.7 all-gather.7.cloned.1.call-update
  7.9 0.0 all-gather.5.cloned.1.call-start
  8.0 0.7 all-gather.5.cloned.1.call-update
  8.7 0.7 copy.14
  9.4 32.6 %all_gather.18 = bf16[1,16,4096]{2,0,1:T(2,128)(2,1)S(1)} all-gather(bf16[1,2,4096]{2,0,1:T(2,128)(2,1)S(1)} %copy.14), channel_id=1, replica_groups=mesh['tp'=8,'dp'=4] {'tp'}, dimensions={1}, use_global_device_ids=true | all-gather | bytes 147456 | tf_op jit(solution)/shard_map/all_gather | solution.py:17
  42.0 0.1 copy.18
  42.1 1.2 dynamic-slice
  44.0 10.5 %all_gather.22 = bf16[4,16,4096]{2,1,0:T(8,128)(2,1)S(1)} all-gather(bf16[1,16,4096]{2,1,0:T(8,128)(2,1)S(1)} %copy.18), channel_id=1, replica_groups=mesh['tp'=8,'dp'=4] {'dp'}, dimensions={0}, use_global_device_ids=true | all-gather | bytes 655360 | tf_op jit(solution)/shard_map/all_gather | solution.py:37
  54.5 66.5 %all-gather.7.cloned.1.call-done = bf16[4096,2048]{1,0:T(8,128)(2,1)} async-done(((bf16[1024,2048]{1,0:T(8,128)(2,1)}), bf16[4096,2048]{1,0:T(8,128)(2,1)}) %all-gather.7.cloned.1.call-update) | async-done | bytes 16777232 | tf_op jit(solution)/shard_map/all_gather | solution.py:15
  121.0 8.0 %fusion.3 = f32[16,2048]{1,0:T(8,128)S(1)} fusion(bf16[4096,2048]{1,0:T(8,128)(2,1)} %all-gather.7.cloned.1.call-done, bf16[1,16,4096]{2,1,0:T(8,128)(2,1)S(1)} %copy.18), kind=kOutput, calls=%fused_computation.20 | convolution fusion | flops 268435456 | bytes 17039360 | tf_op jit(solution)/shard_map/dot_general | solution.py:20
  129.0 99.4 %all-gather.5.cloned.1.call-done = bf16[4096,2048]{1,0:T(8,128)(2,1)} async-done(((bf16[1024,2048]{1,0:T(8,128)(2,1)}), bf16[4096,2048]{1,0:T(8,128)(2,1)}) %all-gather.5.cloned.1.call-update) | async-done | bytes 16777232 | tf_op jit(solution)/shard_map/all_gather | solution.py:14
  228.5 0.0 copy-done
  228.5 8.7 %fusion.1 = (bf16[16,2048]{1,0:T(8,128)(2,1)S(1)}, bf16[1,16,2048]{2,1,0:T(8,128)(2,1)}, bf16[16,2048]{1,0:T(8,128)(2,1)S(1)}) fusion(f32[16,2048]{1,0:T(8,128)S(1)} %fusion.3, bf16[1,16,2048]{2,1,0:T(8,128)(2,1)S(1)} %copy-done, bf16[4096,2048]{1,0:T(8,128)(2,1)} %all-gather.5.cloned.1.call-done, bf16[1,16,4096]{2,1,0:T(8,128)(2,1)S(1)} %copy.18), kind=kOutput, calls=%fused_computation.14 | convolution fusion | flops 268959744 | bytes 17301504 | tf_op jit(solution)/shard_map/dot_general | solution.py:19
  237.2 5.9 %all-gather.1 = bf16[64,2048]{1,0:T(8,128)(2,1)S(1)} all-gather(bf16[16,2048]{1,0:T(8,128)(2,1)S(1)} %get-tuple-element.18), channel_id=3, replica_groups=mesh['tp'=8,'dp'=4] {'dp'}, dimensions={0}, use_global_device_ids=true | all-gather | bytes 327680 | tf_op jit(solution)/shard_map/all_gather | solution.py:39
  243.1 8.5 %convert_bitcast_fusion = bf16[4096,2048]{0,1:T(8,128)(2,1)} fusion(bf16[4,16,4096]{2,1,0:T(8,128)(2,1)S(1)} %all_gather.22, bf16[64,2048]{1,0:T(8,128)(2,1)S(1)} %all-gather.1), kind=kOutput, calls=%fused_computation.2 | convolution fusion | flops 276824064 | bytes 16973824 | tf_op jit(solution)/shard_map/dot_general | solution.py:46
  251.7 8.1 %convert_bitcast_fusion.1 = bf16[4096,2048]{0,1:T(8,128)(2,1)} fusion(bf16[4,16,4096]{2,1,0:T(8,128)(2,1)S(1)} %all_gather.22, bf16[64,2048]{1,0:T(8,128)(2,1)S(1)} %all-gather.1), kind=kOutput, calls=%fused_computation.3 | convolution fusion | flops 276824064 | bytes 16973824 | tf_op jit(solution)/shard_map/dot_general | solution.py:46
  259.7 8.0 %convert_bitcast_fusion.2 = bf16[4096,2048]{0,1:T(8,128)(2,1)} fusion(bf16[4,16,4096]{2,1,0:T(8,128)(2,1)S(1)} %all_gather.22, bf16[64,2048]{1,0:T(8,128)(2,1)S(1)} %all-gather.1), kind=kOutput, calls=%fused_computation.4 | convolution fusion | flops 276824064 | bytes 16973824 | tf_op jit(solution)/shard_map/dot_general | solution.py:46
  267.8 8.0 %convert_bitcast_fusion.3 = bf16[4096,2048]{0,1:T(8,128)(2,1)} fusion(bf16[4,16,4096]{2,1,0:T(8,128)(2,1)S(1)} %all_gather.22, bf16[64,2048]{1,0:T(8,128)(2,1)S(1)} %all-gather.1), kind=kOutput, calls=%fused_computation.5 | convolution fusion | flops 276824064 | bytes 16973824 | tf_op jit(solution)/shard_map/dot_general | solution.py:46
  275.8 6.0 %all-gather = bf16[64,2048]{1,0:T(8,128)(2,1)S(1)} all-gather(bf16[16,2048]{1,0:T(8,128)(2,1)S(1)} %get-tuple-element.16), channel_id=2, replica_groups=mesh['tp'=8,'dp'=4] {'dp'}, dimensions={0}, use_global_device_ids=true | all-gather | bytes 327680 | tf_op jit(solution)/shard_map/all_gather | solution.py:38
  281.9 8.5 %convert_bitcast_fusion.4 = bf16[4096,2048]{0,1:T(8,128)(2,1)} fusion(bf16[4,16,4096]{2,1,0:T(8,128)(2,1)S(1)} %all_gather.22, bf16[64,2048]{1,0:T(8,128)(2,1)S(1)} %all-gather), kind=kOutput, calls=%fused_computation.6 | convolution fusion | flops 276824064 | bytes 16973824 | tf_op jit(solution)/shard_map/dot_general | solution.py:43
  290.4 8.1 %convert_bitcast_fusion.5 = bf16[4096,2048]{0,1:T(8,128)(2,1)} fusion(bf16[4,16,4096]{2,1,0:T(8,128)(2,1)S(1)} %all_gather.22, bf16[64,2048]{1,0:T(8,128)(2,1)S(1)} %all-gather), kind=kOutput, calls=%fused_computation.7 | convolution fusion | flops 276824064 | bytes 16973824 | tf_op jit(solution)/shard_map/dot_general | solution.py:43
  298.5 8.1 %convert_bitcast_fusion.6 = bf16[4096,2048]{0,1:T(8,128)(2,1)} fusion(bf16[4,16,4096]{2,1,0:T(8,128)(2,1)S(1)} %all_gather.22, bf16[64,2048]{1,0:T(8,128)(2,1)S(1)} %all-gather), kind=kOutput, calls=%fused_computation.8 | convolution fusion | flops 276824064 | bytes 16973824 | tf_op jit(solution)/shard_map/dot_general | solution.py:43
  306.5 8.1 %convert_bitcast_fusion.7 = bf16[4096,2048]{0,1:T(8,128)(2,1)} fusion(bf16[4,16,4096]{2,1,0:T(8,128)(2,1)S(1)} %all_gather.22, bf16[64,2048]{1,0:T(8,128)(2,1)S(1)} %all-gather), kind=kOutput, calls=%fused_computation.9 | convolution fusion | flops 276824064 | bytes 16973824 | tf_op jit(solution)/shard_map/dot_general | solution.py:43
  314.6 10.2 %fusion.20 = f32[16,4096]{1,0:T(8,128)S(1)} fusion(bf16[16,2048]{1,0:T(8,128)(2,1)S(1)} %get-tuple-element.16, bf16[4096,2048]{1,0:T(8,128)(2,1)} %all-gather.5.cloned.1.call-done), kind=kOutput, calls=%fused_computation.38 | convolution fusion | flops 268435456 | bytes 17104896 | tf_op jit(solution)/shard_map/dot_general | solution.py:28
  324.8 10.2 %convolution_add_fusion = f32[16,4096]{1,0:T(8,128)S(1)} fusion(f32[16,4096]{1,0:T(8,128)S(1)} %fusion.20, bf16[16,2048]{1,0:T(8,128)(2,1)S(1)} %get-tuple-element.18, bf16[4096,2048]{1,0:T(8,128)(2,1)} %all-gather.7.cloned.1.call-done), kind=kOutput, calls=%fused_computation.10 | convolution fusion | flops 268500992 | bytes 17367040 | tf_op jit(solution)/shard_map/dot_general | solution.py:30
  335.0 40.4 %all-reduce.2 = bf16[16,4096]{1,0:T(8,128)(2,1)S(1)} all-reduce(f32[16,4096]{1,0:T(8,128)S(1)} %convolution_add_fusion), channel_id=4, replica_groups=mesh['tp'=8,'dp'=4] {'tp'}, use_global_device_ids=true, to_apply=%region_0.0.clone | all-reduce | flops 65536 | bytes 393216
  375.4 28.7 %multiply_convert_fusion = bf16[4096,2048]{0,1:T(8,128)(2,1)} fusion(bf16[4096,2048]{0,1:T(8,128)(2,1)} %convert_bitcast_fusion, bf16[4096,2048]{0,1:T(8,128)(2,1)} %convert_bitcast_fusion.1, bf16[4096,2048]{0,1:T(8,128)(2,1)} %convert_bitcast_fusion.2, bf16[4096,2048]{0,1:T(8,128)(2,1)} %convert_bitcast_fusion.3), kind=kLoop, calls=%fused_computation | loop fusion | flops 75497472 | bytes 83886080 | tf_op jit(solution)/shard_map/convert_element_type | solution.py:54
  404.2 22.4 %copy.17 = bf16[4096,2048]{1,0:T(8,128)(2,1)} copy(bf16[4096,2048]{0,1:T(8,128)(2,1)} %multiply_convert_fusion) | data formatting | bytes 33554432
  426.6 28.8 %multiply_convert_fusion.1 = bf16[4096,2048]{0,1:T(8,128)(2,1)} fusion(bf16[4096,2048]{0,1:T(8,128)(2,1)} %convert_bitcast_fusion.4, bf16[4096,2048]{0,1:T(8,128)(2,1)} %convert_bitcast_fusion.5, bf16[4096,2048]{0,1:T(8,128)(2,1)} %convert_bitcast_fusion.6, bf16[4096,2048]{0,1:T(8,128)(2,1)} %convert_bitcast_fusion.7), kind=kLoop, calls=%fused_computation.1 | loop fusion | flops 75497472 | bytes 83886080 | tf_op jit(solution)/shard_map/convert_element_type | solution.py:53
  455.3 22.4 %copy.16 = bf16[4096,2048]{1,0:T(8,128)(2,1)} copy(bf16[4096,2048]{0,1:T(8,128)(2,1)} %multiply_convert_fusion.1) | data formatting | bytes 33554432
  477.8 0.6 fusion.17
Async XLA Ops:
  7.2 221.3 %copy-start = (bf16[1,16,2048]{2,1,0:T(8,128)(2,1)S(1)}, bf16[1,16,2048]{2,1,0:T(8,128)(2,1)}, u32[]{:S(2)}) copy-start(bf16[1,16,2048]{2,1,0:T(8,128)(2,1)} %param.7) | copy-start | bytes 196612
  7.2 113.8 %all-gather.7.cloned.1.call-start = ((), (), s32[]{:S(2)}) async-start(), calls=%async_computation.1 | async-start | bytes 20971520 | tf_op jit(solution)/shard_map/all_gather | solution.py:15
  7.9 220.6 %all-gather.5.cloned.1.call-start = ((), (), s32[]{:S(2)}) async-start(), calls=%async_computation | async-start | bytes 20971520 | tf_op jit(solution)/shard_map/all_gather | solution.py:14
Sparse Core Ops, SparseCore 0:
  9.5 111.4 all-gather.6
  122.6 105.8 all-gather.4
where the time goes:
time: 487 us; the launch traced here: 485 us
  waiting for transfers between devices  167 us (34%)
  matrix products  103 us (21%)
  blocking collectives  95.5 us (20%)
  other arithmetic  57.5 us (12%)
  local copies, waits for them, and re-layouts  47.6 us (10%)
  between operations  14.7 us (3%)
    all_gather x1, waiting for transfers between devices, shards(): lax.all_gather(gate_weight, 'dp', axis=0, tiled=True)  99.4 us
    all_gather x1, waiting for transfers between devices, shards(): lax.all_gather(up_weight, 'dp', axis=0, tiled=True)  66.5 us
    unnamed x7, local copies, waits for them, and re-layouts  47 us
    unnamed x1, blocking collectives  40.4 us
    dot_general x4, matrix products, shards(): lax.dot_general(rows_p[replica], gate_p[replica], down_rows, preferred_el...  32.7 us
    dot_general x4, matrix products, shards(): lax.dot_general(rows_p[replica], up_p[replica], down_rows, preferred_elem...  32.7 us
    all_gather x1, blocking collectives, shards(): gathered = lax.all_gather(tokens, 'tp', axis=1, tiled=True)  32.6 us
    convert_element_type x1, other arithmetic, shards(): grad_gate = (acc_gate * inverse_dp).astype(jnp.bfloat16)  28.8 us
  transfers between devices with their start and end apart: 2, of which 2 were waited for; matrix products, arithmetic and copies ran while one was open for 2% of the time, Pallas kernels for 0%

commit v1 on v0

--- a/solution.py
+++ b/solution.py
@@ -14,7 +14,12 @@
         lax.all_gather(gate_weight, "dp", axis=0, tiled=True),
         lax.all_gather(up_weight, "dp", axis=0, tiled=True),
     )
-    gathered = lax.all_gather(tokens, "tp", axis=1, tiled=True)
+    ring = [tokens]
+    for hop in range(7):
+        ring.append(lax.ppermute(ring[-1], "tp", [(dev, (dev + 1) % 8) for dev in range(8)]))
+    gathered = jnp.roll(
+        jnp.concatenate(ring[::-1], axis=1), (lax.axis_index("tp") + 1) * ring[0].shape[1], axis=1
+    )
     flat_rows = gathered[0]
     gate_pre = jnp.dot(flat_rows, gate_full, preferred_element_type=jnp.float32)
     up_pre = jnp.dot(flat_rows, up_full, preferred_element_type=jnp.float32)

time: 487 us -> 445 us (0.914)
  local copies, waits for them, and re-layouts: 47.6 us -> 3.74 us
  blocking collectives: 95.5 us -> 63 us
  waiting for transfers between devices: 167 us -> 196 us
    all_gather x1, waiting for transfers between devices: 99.4 us -> 53.3 us  [shards(): lax.all_gather(gate_weight, 'dp', axis=0, tiled=True)]
    unnamed x7 -> x3, local copies, waits for them, and re-layouts: 47 us -> 1.24 us
    ppermute x0 -> x7, waiting for transfers between devices: none -> 41.7 us  [shards(): lax.ppermute(ring[-1], 'tp', [(dev, (dev + 1) % 8) for dev in range(8)])]
    all_gather x1, waiting for transfers between devices: 66.5 us -> 99.4 us  [shards(): lax.all_gather(up_weight, 'dp', axis=0, tiled=True)]
    all_gather x1 -> x0, blocking collectives: 32.6 us -> none  [shards(): gathered = lax.all_gather(tokens, 'tp', axis=1, tiled=True)]
  transfers between devices with their start and end apart: 2 -> 9, of which waited for: 2 -> 9; matrix products, arithmetic and copies ran while one was open for 2% -> 3% of each run, Pallas kernels for 0% -> 0%
where the time goes in v1:
time: 445 us; the launch traced here: 444 us
  waiting for transfers between devices  196 us (44%)
  matrix products  103 us (23%)
  blocking collectives  63 us (14%)
  other arithmetic  61 us (14%)
  between operations  14.7 us (3%)
    all_gather x1, waiting for transfers between devices, shards(): lax.all_gather(up_weight, 'dp', axis=0, tiled=True)  99.4 us
    all_gather x1, waiting for transfers between devices, shards(): lax.all_gather(gate_weight, 'dp', axis=0, tiled=True)  53.3 us
    ppermute x7, waiting for transfers between devices, shards(): lax.ppermute(ring[-1], 'tp', [(dev, (dev + 1) % 8) for dev in range(8)])  41.7 us
    unnamed x1, blocking collectives  40.4 us
    dot_general x4, matrix products, shards(): lax.dot_general(rows_p[replica], up_p[replica], down_rows, preferred_elem...  32.9 us
    dot_general x4, matrix products, shards(): lax.dot_general(rows_p[replica], gate_p[replica], down_rows, preferred_el...  32.9 us
    convert_element_type x1, other arithmetic, shards(): grad_gate = (acc_gate * inverse_dp).astype(jnp.bfloat16)  30.5 us
    convert_element_type x1, other arithmetic, shards(): grad_up = (acc_up * inverse_dp).astype(jnp.bfloat16)  30.5 us
  transfers between devices with their start and end apart: 9, of which 9 were waited for; matrix products, arithmetic and copies ran while one was open for 3% of the time, Pallas kernels for 0%

profile of v1, /device:TPU:0, one launch (start us, length us, event | category | flops | bytes accessed | tf_op | source)
XLA Modules:
  0.0 444.3 jit_solution(15107727376023341547)
XLA Ops:
  7.2 0.0 copy-start
  7.2 0.0 all-gather.5.cloned.1.call-start
  7.2 0.7 all-gather.5.cloned.1.call-update
  7.9 0.0 all-gather.7.cloned.1.call-start
  8.0 0.7 all-gather.7.cloned.1.call-update
  8.7 3.0 collective-permute-start
  11.7 5.0 %collective-permute-done = bf16[1,2,4096]{2,1,0:T(2,128)(2,1)S(1)} collective-permute-done((bf16[1,2,4096]{2,1,0:T(2,128)(2,1)}, bf16[1,2,4096]{2,1,0:T(2,128)(2,1)S(1)}, u32[]{:S(2)}, u32[]{:S(2)}) %collective-permute-start) | collective-permute-done | bytes 16416 | tf_op jit(solution)/shard_map/ppermute | solution.py:19
  16.7 0.0 collective-permute-start.1
  16.7 6.4 %collective-permute-done.1 = bf16[1,2,4096]{2,1,0:T(2,128)(2,1)S(1)} collective-permute-done((bf16[1,2,4096]{2,1,0:T(2,128)(2,1)S(1)}, bf16[1,2,4096]{2,1,0:T(2,128)(2,1)S(1)}, u32[]{:S(2)}, u32[]{:S(2)}) %collective-permute-start.1) | collective-permute-done | bytes 16416 | tf_op jit(solution)/shard_map/ppermute | solution.py:19
  23.1 0.0 collective-permute-start.2
  23.1 6.4 %collective-permute-done.2 = bf16[1,2,4096]{2,1,0:T(2,128)(2,1)S(1)} collective-permute-done((bf16[1,2,4096]{2,1,0:T(2,128)(2,1)S(1)}, bf16[1,2,4096]{2,1,0:T(2,128)(2,1)S(1)}, u32[]{:S(2)}, u32[]{:S(2)}) %collective-permute-start.2) | collective-permute-done | bytes 16416 | tf_op jit(solution)/shard_map/ppermute | solution.py:19
  29.5 0.0 collective-permute-start.3
  29.6 6.4 %collective-permute-done.3 = bf16[1,2,4096]{2,1,0:T(2,128)(2,1)S(1)} collective-permute-done((bf16[1,2,4096]{2,1,0:T(2,128)(2,1)S(1)}, bf16[1,2,4096]{2,1,0:T(2,128)(2,1)S(1)}, u32[]{:S(2)}, u32[]{:S(2)}) %collective-permute-start.3) | collective-permute-done | bytes 16416 | tf_op jit(solution)/shard_map/ppermute | solution.py:19
  36.0 0.0 collective-permute-start.4
  36.0 6.4 %collective-permute-done.4 = bf16[1,2,4096]{2,1,0:T(2,128)(2,1)S(1)} collective-permute-done((bf16[1,2,4096]{2,1,0:T(2,128)(2,1)S(1)}, bf16[1,2,4096]{2,1,0:T(2,128)(2,1)S(1)}, u32[]{:S(2)}, u32[]{:S(2)}) %collective-permute-start.4) | collective-permute-done | bytes 16416 | tf_op jit(solution)/shard_map/ppermute | solution.py:19
  42.4 0.0 collective-permute-start.5
  42.4 6.4 %collective-permute-done.5 = bf16[1,2,4096]{2,1,0:T(2,128)(2,1)S(1)} collective-permute-done((bf16[1,2,4096]{2,1,0:T(2,128)(2,1)S(1)}, bf16[1,2,4096]{2,1,0:T(2,128)(2,1)S(1)}, u32[]{:S(2)}, u32[]{:S(2)}) %collective-permute-start.5) | collective-permute-done | bytes 16416 | tf_op jit(solution)/shard_map/ppermute | solution.py:19
  48.9 0.0 collective-permute-start.6
  48.9 1.2 dynamic-slice
  50.8 4.5 %collective-permute-done.6 = bf16[1,2,4096]{2,1,0:T(2,128)(2,1)S(1)} collective-permute-done((bf16[1,2,4096]{2,1,0:T(2,128)(2,1)S(1)}, bf16[1,2,4096]{2,1,0:T(2,128)(2,1)S(1)}, u32[]{:S(2)}, u32[]{:S(2)}) %collective-permute-start.6) | collective-permute-done | bytes 16416 | tf_op jit(solution)/shard_map/ppermute | solution.py:19
  55.3 1.8 concatenate.6
  57.2 10.6 %all_gather.17 = bf16[4,16,4096]{2,1,0:T(8,128)(2,1)S(1)} all-gather(bf16[1,16,4096]{2,1,0:T(8,128)(2,1)S(1)} %constant_dynamic-slice_fusion), channel_id=1, replica_groups=mesh['tp'=8,'dp'=4] {'dp'}, dimensions={0}, use_global_device_ids=true | all-gather | bytes 655360 | tf_op jit(solution)/shard_map/all_gather | solution.py:42
  67.7 53.3 %all-gather.5.cloned.1.call-done = bf16[4096,2048]{1,0:T(8,128)(2,1)} async-done(((bf16[1024,2048]{1,0:T(8,128)(2,1)}), bf16[4096,2048]{1,0:T(8,128)(2,1)}) %all-gather.5.cloned.1.call-update) | async-done | bytes 16777232 | tf_op jit(solution)/shard_map/all_gather | solution.py:14
  121.0 8.0 %fusion.5 = f32[16,2048]{1,0:T(8,128)S(1)} fusion(bf16[4096,2048]{1,0:T(8,128)(2,1)} %all-gather.5.cloned.1.call-done, bf16[1,16,4096]{2,1,0:T(8,128)(2,1)S(1)} %constant_dynamic-slice_fusion), kind=kOutput, calls=%fused_computation.22 | convolution fusion | flops 268435456 | bytes 17039360 | tf_op jit(solution)/shard_map/dot_general | solution.py:24
  129.0 99.4 %all-gather.7.cloned.1.call-done = bf16[4096,2048]{1,0:T(8,128)(2,1)} async-done(((bf16[1024,2048]{1,0:T(8,128)(2,1)}), bf16[4096,2048]{1,0:T(8,128)(2,1)}) %all-gather.7.cloned.1.call-update) | async-done | bytes 16777232 | tf_op jit(solution)/shard_map/all_gather | solution.py:15
  228.5 0.0 copy-done
  228.5 8.7 %fusion.1 = (bf16[16,2048]{1,0:T(8,128)(2,1)S(1)}, bf16[1,16,2048]{2,1,0:T(8,128)(2,1)}, bf16[16,2048]{1,0:T(8,128)(2,1)S(1)}) fusion(f32[16,2048]{1,0:T(8,128)S(1)} %fusion.5, bf16[1,16,2048]{2,1,0:T(8,128)(2,1)S(1)} %copy-done, bf16[4096,2048]{1,0:T(8,128)(2,1)} %all-gather.7.cloned.1.call-done, bf16[1,16,4096]{2,1,0:T(8,128)(2,1)S(1)} %constant_dynamic-slice_fusion), kind=kOutput, calls=%fused_computation.14 | convolution fusion | flops 268959744 | bytes 17301504 | tf_op jit(solution)/shard_map/dot_general | solution.py:25
  237.2 5.9 %all-gather.1 = bf16[64,2048]{1,0:T(8,128)(2,1)S(1)} all-gather(bf16[16,2048]{1,0:T(8,128)(2,1)S(1)} %get-tuple-element.6), channel_id=3, replica_groups=mesh['tp'=8,'dp'=4] {'dp'}, dimensions={0}, use_global_device_ids=true | all-gather | bytes 327680 | tf_op jit(solution)/shard_map/all_gather | solution.py:44
  243.1 8.5 %convolution_convert_fusion = bf16[4096,2048]{1,0:T(8,128)(2,1)} fusion(bf16[4,16,4096]{2,1,0:T(8,128)(2,1)S(1)} %all_gather.17, bf16[64,2048]{1,0:T(8,128)(2,1)S(1)} %all-gather.1), kind=kOutput, calls=%fused_computation.2 | convolution fusion | flops 276824064 | bytes 16973824 | tf_op jit(solution)/shard_map/dot_general | solution.py:51
  251.6 8.2 %convolution_convert_fusion.1 = bf16[4096,2048]{1,0:T(8,128)(2,1)} fusion(bf16[4,16,4096]{2,1,0:T(8,128)(2,1)S(1)} %all_gather.17, bf16[64,2048]{1,0:T(8,128)(2,1)S(1)} %all-gather.1), kind=kOutput, calls=%fused_computation.3 | convolution fusion | flops 276824064 | bytes 16973824 | tf_op jit(solution)/shard_map/dot_general | solution.py:51
  259.8 8.1 %convolution_convert_fusion.2 = bf16[4096,2048]{1,0:T(8,128)(2,1)} fusion(bf16[4,16,4096]{2,1,0:T(8,128)(2,1)S(1)} %all_gather.17, bf16[64,2048]{1,0:T(8,128)(2,1)S(1)} %all-gather.1), kind=kOutput, calls=%fused_computation.4 | convolution fusion | flops 276824064 | bytes 16973824 | tf_op jit(solution)/shard_map/dot_general | solution.py:51
  267.9 8.1 %convolution_convert_fusion.3 = bf16[4096,2048]{1,0:T(8,128)(2,1)} fusion(bf16[4,16,4096]{2,1,0:T(8,128)(2,1)S(1)} %all_gather.17, bf16[64,2048]{1,0:T(8,128)(2,1)S(1)} %all-gather.1), kind=kOutput, calls=%fused_computation.5 | convolution fusion | flops 276824064 | bytes 16973824 | tf_op jit(solution)/shard_map/dot_general | solution.py:51
  276.0 6.1 %all-gather = bf16[64,2048]{1,0:T(8,128)(2,1)S(1)} all-gather(bf16[16,2048]{1,0:T(8,128)(2,1)S(1)} %get-tuple-element.4), channel_id=2, replica_groups=mesh['tp'=8,'dp'=4] {'dp'}, dimensions={0}, use_global_device_ids=true | all-gather | bytes 327680 | tf_op jit(solution)/shard_map/all_gather | solution.py:43
  282.1 8.5 %convolution_convert_fusion.4 = bf16[4096,2048]{1,0:T(8,128)(2,1)} fusion(bf16[4,16,4096]{2,1,0:T(8,128)(2,1)S(1)} %all_gather.17, bf16[64,2048]{1,0:T(8,128)(2,1)S(1)} %all-gather), kind=kOutput, calls=%fused_computation.6 | convolution fusion | flops 276824064 | bytes 16973824 | tf_op jit(solution)/shard_map/dot_general | solution.py:48
  290.6 8.1 %convolution_convert_fusion.5 = bf16[4096,2048]{1,0:T(8,128)(2,1)} fusion(bf16[4,16,4096]{2,1,0:T(8,128)(2,1)S(1)} %all_gather.17, bf16[64,2048]{1,0:T(8,128)(2,1)S(1)} %all-gather), kind=kOutput, calls=%fused_computation.7 | convolution fusion | flops 276824064 | bytes 16973824 | tf_op jit(solution)/shard_map/dot_general | solution.py:48
  298.7 8.1 %convolution_convert_fusion.6 = bf16[4096,2048]{1,0:T(8,128)(2,1)} fusion(bf16[4,16,4096]{2,1,0:T(8,128)(2,1)S(1)} %all_gather.17, bf16[64,2048]{1,0:T(8,128)(2,1)S(1)} %all-gather), kind=kOutput, calls=%fused_computation.8 | convolution fusion | flops 276824064 | bytes 16973824 | tf_op jit(solution)/shard_map/dot_general | solution.py:48
  306.8 8.2 %convolution_convert_fusion.7 = bf16[4096,2048]{1,0:T(8,128)(2,1)} fusion(bf16[4,16,4096]{2,1,0:T(8,128)(2,1)S(1)} %all_gather.17, bf16[64,2048]{1,0:T(8,128)(2,1)S(1)} %all-gather), kind=kOutput, calls=%fused_computation.9 | convolution fusion | flops 276824064 | bytes 16973824 | tf_op jit(solution)/shard_map/dot_general | solution.py:48
  315.0 10.2 %fusion.20 = f32[16,4096]{1,0:T(8,128)S(1)} fusion(bf16[16,2048]{1,0:T(8,128)(2,1)S(1)} %get-tuple-element.4, bf16[4096,2048]{1,0:T(8,128)(2,1)} %all-gather.5.cloned.1.call-done), kind=kOutput, calls=%fused_computation.39 | convolution fusion | flops 268435456 | bytes 17104896 | tf_op jit(solution)/shard_map/dot_general | solution.py:33
  325.2 10.2 %convolution_add_fusion = f32[16,4096]{1,0:T(8,128)S(1)} fusion(f32[16,4096]{1,0:T(8,128)S(1)} %fusion.20, bf16[16,2048]{1,0:T(8,128)(2,1)S(1)} %get-tuple-element.6, bf16[4096,2048]{1,0:T(8,128)(2,1)} %all-gather.7.cloned.1.call-done), kind=kOutput, calls=%fused_computation.10 | convolution fusion | flops 268500992 | bytes 17367040 | tf_op jit(solution)/shard_map/dot_general | solution.py:35
  335.4 40.4 %all-reduce.2 = bf16[16,4096]{1,0:T(8,128)(2,1)S(1)} all-reduce(f32[16,4096]{1,0:T(8,128)S(1)} %convolution_add_fusion), channel_id=4, replica_groups=mesh['tp'=8,'dp'=4] {'tp'}, use_global_device_ids=true, to_apply=%region_0.1.clone | all-reduce | flops 65536 | bytes 393216
  375.9 0.6 fusion.17
  376.5 30.5 %multiply_convert_fusion = bf16[4096,2048]{1,0:T(8,128)(2,1)} fusion(bf16[4096,2048]{1,0:T(8,128)(2,1)} %convolution_convert_fusion, bf16[4096,2048]{1,0:T(8,128)(2,1)} %convolution_convert_fusion.1, bf16[4096,2048]{1,0:T(8,128)(2,1)} %convolution_convert_fusion.2, bf16[4096,2048]{1,0:T(8,128)(2,1)} %convolution_convert_fusion.3), kind=kLoop, calls=%fused_computation | loop fusion | flops 75497472 | bytes 83886080 | tf_op jit(solution)/shard_map/convert_element_type | solution.py:59
  407.0 30.5 %multiply_convert_fusion.1 = bf16[4096,2048]{1,0:T(8,128)(2,1)} fusion(bf16[4096,2048]{1,0:T(8,128)(2,1)} %convolution_convert_fusion.4, bf16[4096,2048]{1,0:T(8,128)(2,1)} %convolution_convert_fusion.5, bf16[4096,2048]{1,0:T(8,128)(2,1)} %convolution_convert_fusion.6, bf16[4096,2048]{1,0:T(8,128)(2,1)} %convolution_convert_fusion.7), kind=kLoop, calls=%fused_computation.1 | loop fusion | flops 75497472 | bytes 83886080 | tf_op jit(solution)/shard_map/convert_element_type | solution.py:58
  (1 shorter events, 0.0 us)
Async XLA Ops:
  7.2 221.3 %copy-start = (bf16[1,16,2048]{2,1,0:T(8,128)(2,1)S(1)}, bf16[1,16,2048]{2,1,0:T(8,128)(2,1)}, u32[]{:S(2)}) copy-start(bf16[1,16,2048]{2,1,0:T(8,128)(2,1)} %param.7) | copy-start | bytes 196612
  7.2 113.8 %all-gather.5.cloned.1.call-start = ((), (), s32[]{:S(2)}) async-start(), calls=%async_computation | async-start | bytes 20971520 | tf_op jit(solution)/shard_map/all_gather | solution.py:14
  7.9 220.6 %all-gather.7.cloned.1.call-start = ((), (), s32[]{:S(2)}) async-start(), calls=%async_computation.1 | async-start | bytes 20971520 | tf_op jit(solution)/shard_map/all_gather | solution.py:15
  8.7 8.0 %collective-permute-start = (bf16[1,2,4096]{2,1,0:T(2,128)(2,1)}, bf16[1,2,4096]{2,1,0:T(2,128)(2,1)S(1)}, u32[]{:S(2)}, u32[]{:S(2)}) collective-permute-start(bf16[1,2,4096]{2,1,0:T(2,128)(2,1)} %param.4), channel_id=1, source_target_pairs={{0,4},{4,8},{8,12},{12,16},{16,20},{20,24},{24,28},{28,0},{1,5},{5... | collective-permute-start | bytes 49160 | tf_op jit(solution)/shard_map/ppermute | solution.py:19
  16.7 6.4 %collective-permute-start.1 = (bf16[1,2,4096]{2,1,0:T(2,128)(2,1)S(1)}, bf16[1,2,4096]{2,1,0:T(2,128)(2,1)S(1)}, u32[]{:S(2)}, u32[]{:S(2)}) collective-permute-start(bf16[1,2,4096]{2,1,0:T(2,128)(2,1)S(1)} %collective-permute-done), channel_id=1, source_target_pairs={{0,4},{4,8},{8,12},{12,16},{16,20},{20,24},{24,28},{28,0},{1,5},{5... | collective-permute-start | bytes 49160 | tf_op jit(solution)/shard_map/ppermute | solution.py:19
  23.1 6.4 %collective-permute-start.2 = (bf16[1,2,4096]{2,1,0:T(2,128)(2,1)S(1)}, bf16[1,2,4096]{2,1,0:T(2,128)(2,1)S(1)}, u32[]{:S(2)}, u32[]{:S(2)}) collective-permute-start(bf16[1,2,4096]{2,1,0:T(2,128)(2,1)S(1)} %collective-permute-done.1), channel_id=1, source_target_pairs={{0,4},{4,8},{8,12},{12,16},{16,20},{20,24},{24,28},{28,0},{1,5},{5... | collective-permute-start | bytes 49160 | tf_op jit(solution)/shard_map/ppermute | solution.py:19
  29.5 6.4 %collective-permute-start.3 = (bf16[1,2,4096]{2,1,0:T(2,128)(2,1)S(1)}, bf16[1,2,4096]{2,1,0:T(2,128)(2,1)S(1)}, u32[]{:S(2)}, u32[]{:S(2)}) collective-permute-start(bf16[1,2,4096]{2,1,0:T(2,128)(2,1)S(1)} %collective-permute-done.2), channel_id=1, source_target_pairs={{0,4},{4,8},{8,12},{12,16},{16,20},{20,24},{24,28},{28,0},{1,5},{5... | collective-permute-start | bytes 49160 | tf_op jit(solution)/shard_map/ppermute | solution.py:19
  36.0 6.4 %collective-permute-start.4 = (bf16[1,2,4096]{2,1,0:T(2,128)(2,1)S(1)}, bf16[1,2,4096]{2,1,0:T(2,128)(2,1)S(1)}, u32[]{:S(2)}, u32[]{:S(2)}) collective-permute-start(bf16[1,2,4096]{2,1,0:T(2,128)(2,1)S(1)} %collective-permute-done.3), channel_id=1, source_target_pairs={{0,4},{4,8},{8,12},{12,16},{16,20},{20,24},{24,28},{28,0},{1,5},{5... | collective-permute-start | bytes 49160 | tf_op jit(solution)/shard_map/ppermute | solution.py:19
  42.4 6.4 %collective-permute-start.5 = (bf16[1,2,4096]{2,1,0:T(2,128)(2,1)S(1)}, bf16[1,2,4096]{2,1,0:T(2,128)(2,1)S(1)}, u32[]{:S(2)}, u32[]{:S(2)}) collective-permute-start(bf16[1,2,4096]{2,1,0:T(2,128)(2,1)S(1)} %collective-permute-done.4), channel_id=1, source_target_pairs={{0,4},{4,8},{8,12},{12,16},{16,20},{20,24},{24,28},{28,0},{1,5},{5... | collective-permute-start | bytes 49160 | tf_op jit(solution)/shard_map/ppermute | solution.py:19
  48.9 6.4 %collective-permute-start.6 = (bf16[1,2,4096]{2,1,0:T(2,128)(2,1)S(1)}, bf16[1,2,4096]{2,1,0:T(2,128)(2,1)S(1)}, u32[]{:S(2)}, u32[]{:S(2)}) collective-permute-start(bf16[1,2,4096]{2,1,0:T(2,128)(2,1)S(1)} %collective-permute-done.5), channel_id=1, source_target_pairs={{0,4},{4,8},{8,12},{12,16},{16,20},{20,24},{24,28},{28,0},{1,5},{5... | collective-permute-start | bytes 49160 | tf_op jit(solution)/shard_map/ppermute | solution.py:19
Sparse Core Ops, SparseCore 0:
  9.5 111.4 all-gather.4
  122.6 105.8 all-gather.6
